TPU v7x, 512 devices: a whole 4x8x8 slice. The times are simulated.
512 devices in a mesh: field: 64 (over z, y), batch: 8 (over x, core).
Axes of the slice: x: 4, y: 8, z: 8, core: 2. Of those that a mesh axis runs over, the one named last changes fastest.
Arguments:
- pooled: bfloat16 [4096, 64, 1024], P('batch', 'field'), may hold values from -6 to 6
- counts: int32 [4096, 64], P('batch', 'field'), may hold values from 1 to 16
- w_pairs: bfloat16 [64, 504, 1024], P('field', None, 'batch'), may hold values from -0.03125 to 0.03125
- bias_terms: bfloat16 [1024], P('batch'), may hold values from -4 to 4
- grad_act: bfloat16 [4096, 1024], P('batch'), may hold values from -6 to 6
Outputs:
- entry_grad: bfloat16 [4096, 64, 1024], P('batch', 'field')
- weight_grad: float32 [64, 504, 1024], P('field', None, 'batch')
All inputs are finite; a program needn't handle non-finite values.
Results may differ from a plain program's by a relative error of at most 0.014.
Values may be sent and summed in bfloat16 or wider, within the bound.
No kernel may reach another device: no remote copies, remote signals or barrier semaphores. Data moves between devices by JAX's collectives and lax.ppermute only.
A program may use at most 64 MiB of HBM per device.

v0:
```python
import jax
import jax.numpy as jnp
from jax import lax
from jax.sharding import PartitionSpec as P


def body(pooled, counts, w_pairs, bias_terms, grad_act):
    sample_rows = pooled.shape[0]
    fields = lax.axis_size("field")
    shards = lax.axis_size("batch")
    depth = pooled.shape[2] // fields
    half_depth = depth // 2
    hidden_units = grad_act.shape[1]
    pair_count = w_pairs.shape[1]
    own_rows = sample_rows // fields
    my_field = lax.axis_index("field")
    f32, bf16 = (jnp.float32, jnp.bfloat16)
    embedded = pooled.reshape(sample_rows, fields, depth).transpose(1, 2, 0)
    partner = jnp.arange(fields, dtype=jnp.int32)[:, None, None]
    upper_half = partner < my_field
    mine = jnp.where(upper_half, embedded[:, half_depth:], embedded[:, :half_depth])
    outbound = jnp.where(upper_half, embedded[:, :half_depth], embedded[:, half_depth:])
    received = lax.all_to_all(outbound, "field", split_axis=0, concat_axis=0, tiled=True)
    bias_rows = jnp.pad(bias_terms[None, :], ((0, 0), (0, 0)))
    weight_bias = lax.all_gather(
        jnp.concatenate([w_pairs[0], bias_rows], 0), "batch", axis=1, tiled=True
    )
    weight_cols = weight_bias[:pair_count]
    bias_float = weight_bias[pair_count].astype(f32)
    received_wide = received.astype(f32)
    mine_wide = mine.astype(f32)
    product_all = (mine_wide * received_wide).astype(bf16)
    slot_index = jnp.arange(fields - 1, dtype=jnp.int32)[:, None, None]
    pair_rows = jnp.where(slot_index >= my_field, product_all[1:], product_all[:-1])
    pair_rows = pair_rows.reshape(pair_count, sample_rows)
    partial_hidden = lax.dot_general(
        pair_rows, weight_cols, (((0,), (0,)), ((), ())), preferred_element_type=f32
    )
    shares = lax.all_to_all(
        partial_hidden.astype(bf16).reshape(fields, own_rows, hidden_units),
        "field",
        split_axis=0,
        concat_axis=0,
        tiled=True,
    )
    preact = jnp.sum(shares.astype(f32), 0) + bias_float[None, :]
    gate_value = jax.nn.sigmoid(preact)
    own_grad = lax.dynamic_slice(grad_act, (my_field * own_rows, 0), (own_rows, hidden_units))
    own_slope = (own_grad.astype(f32) * gate_value * (1.0 + preact * (1.0 - gate_value))).astype(
        bf16
    )
    slope_act = lax.all_to_all(
        jnp.broadcast_to(own_slope[None], (fields, own_rows, hidden_units)),
        "field",
        split_axis=0,
        concat_axis=0,
        tiled=True,
    ).reshape(sample_rows, hidden_units)
    pair_grad = lax.dot_general(
        weight_cols, slope_act, (((1,), (1,)), ((), ())), preferred_element_type=f32
    ).reshape(fields - 1, half_depth, sample_rows)
    zero_slot = jnp.zeros((1, half_depth, sample_rows), f32)
    below_slots = jnp.concatenate([pair_grad, zero_slot], 0)
    above_slots = jnp.concatenate([zero_slot, pair_grad], 0)
    dense_grad = jnp.where(
        partner < my_field, below_slots, jnp.where(partner > my_field, above_slots, 0.0)
    )
    returned = lax.all_to_all(
        (dense_grad * mine_wide).astype(bf16), "field", split_axis=0, concat_axis=0, tiled=True
    ).astype(f32)
    weight_term = lax.dot_general(
        pair_rows, slope_act, (((1,), (0,)), ((), ())), preferred_element_type=f32
    ).astype(bf16)
    unit_cols = hidden_units // shards
    weight_shares = lax.all_to_all(
        weight_term.reshape(pair_count, shards, unit_cols).transpose(1, 0, 2),
        "batch",
        split_axis=0,
        concat_axis=0,
        tiled=True,
    )
    weight_grad = jnp.sum(weight_shares.astype(f32), 0)
    local_part = dense_grad * received_wide
    full_grad = jnp.concatenate(
        [jnp.where(upper_half, returned, local_part), jnp.where(upper_half, local_part, returned)],
        1,
    )
    full_grad = full_grad / jnp.sqrt(counts[:, 0].astype(f32))[None, None, :]
    entry_grad = full_grad.astype(bf16).reshape(fields * depth, sample_rows).T
    return (entry_grad[:, None, :], weight_grad[None])


def solution(mesh):
    in_specs = (
        P("batch", "field", None),
        P("batch", "field"),
        P("field", None, "batch"),
        P("batch"),
        P("batch", None),
    )
    out_specs = (P("batch", "field", None), P("field", None, "batch"))
    return jax.shard_map(body, mesh=mesh, in_specs=in_specs, out_specs=out_specs, check_vma=False)
```

profile of v0, /device:TPU:8, one launch (start us, length us, event | category | flops | bytes accessed | tf_op | source)
XLA Modules:
  0.0 168.9 jit_solution(5860360318695180854)
XLA Ops:
  0.6 0.0 copy-start.2
  0.7 0.0 copy-start.4
  0.7 1.5 copy.9
  2.2 0.9 broadcast_select_fusion
  3.2 16.6 %all-to-all-start = ((bf16[64,8,512]{2,1,0:T(8,128)(2,1)}), bf16[64,8,512]{2,1,0:T(8,128)(2,1)S(1)}, u32[]{:S(2)}, u32[]{:S(2)}) async-start(bf16[64,8,512]{2,1,0:T(8,128)(2,1)} %broadcast_select_fusion), calls=%async_computation | async-start | bytes 1048576 | tf_op jit(solution)/shard_map/all_to_all | solution.py:23
  19.8 0.0 copy-done.2
  19.8 0.0 copy-done.4
  19.8 14.6 %all_gather.3 = bf16[505,1024]{1,0:T(8,128)(2,1)S(1)} all-gather(bf16[505,128]{1,0:T(8,128)(2,1)S(1)} %pad_maximum_fusion.1), channel_id=1, replica_groups=mesh['field'=64,'batch'=8] {'batch'}, dimensions={1}, use_global_device_ids=true | all-gather | bytes 1163520 | tf_op jit(solution)/shard_map/all_gather | solution.py:25
  34.4 4.7 %all-to-all-done = bf16[64,8,512]{2,1,0:T(8,128)(2,1)S(1)} async-done(((bf16[64,8,512]{2,1,0:T(8,128)(2,1)}), bf16[64,8,512]{2,1,0:T(8,128)(2,1)S(1)}, u32[]{:S(2)}, u32[]{:S(2)}) %all-to-all-start) | async-done | bytes 524320 | tf_op jit(solution)/shard_map/all_to_all | solution.py:23
  39.1 0.3 fusion.3
  39.4 1.8 %fusion = bf16[64,8,1024]{2,1,0:T(8,128)(2,1)} fusion(bf16[505,1024]{1,0:T(8,128)(2,1)S(1)} %all_gather.3, bf16[64,8,512]{2,1,0:T(8,128)(2,1)S(1)} %fusion.3, pred[63]{0:T(512)(128)(4,1)S(1)} %iota_compare_fusion.1), kind=kOutput, calls=%fused_computation.6 | convolution fusion | flops 529264640 | bytes 3113472 | tf_op jit(solution)/shard_map/dot_general | solution.py:36
  41.2 8.0 %all-to-all-start.1 = ((bf16[64,8,1024]{2,1,0:T(8,128)(2,1)}), bf16[64,8,1024]{2,1,0:T(8,128)(2,1)S(1)}, u32[]{:S(2)}, u32[]{:S(2)}) async-start(bf16[64,8,1024]{2,1,0:T(8,128)(2,1)} %fusion), calls=%async_computation.1 | async-start | bytes 2097152 | tf_op jit(solution)/shard_map/all_to_all | solution.py:39
  49.2 0.7 slice_convert_fusion
  50.0 29.0 %all-to-all-done.1 = bf16[64,8,1024]{2,1,0:T(8,128)(2,1)S(1)} async-done(((bf16[64,8,1024]{2,1,0:T(8,128)(2,1)}), bf16[64,8,1024]{2,1,0:T(8,128)(2,1)S(1)}, u32[]{:S(2)}, u32[]{:S(2)}) %all-to-all-start.1) | async-done | bytes 1048608 | tf_op jit(solution)/shard_map/all_to_all | solution.py:39
  79.0 0.2 convert_reduce_fusion
  79.2 0.7 multiply_convert_fusion
  79.9 0.1 broadcast_in_dim.66
  80.0 35.8 %all_to_all.25 = bf16[64,8,1024]{2,1,0:T(8,128)(2,1)S(1)} all-to-all(bf16[64,8,1024]{2,1,0:T(8,128)(2,1)S(1)} %broadcast_in_dim.66), channel_id=1, replica_groups=mesh['field'=64,'batch'=8] {'field'}, dimensions={0} | all-to-all | bytes 2097152 | tf_op jit(solution)/shard_map/all_to_all | solution.py:52
  115.9 0.7 fusion.1
  116.6 1.2 copy.14
  117.8 4.2 %all-to-all-start.4 = ((bf16[8,504,128]{2,1,0:T(8,128)(2,1)}), bf16[8,504,128]{2,1,0:T(8,128)(2,1)}, u32[]{:S(2)}, u32[]{:S(2)}) async-start(bf16[8,504,128]{2,1,0:T(8,128)(2,1)} %bitcast.36), calls=%async_computation.4 | async-start | bytes 2064384 | tf_op jit(solution)/shard_map/all_to_all | solution.py:75
  122.1 2.3 %fusion.4 = f32[63,8,512]{2,1,0:T(8,128)S(1)} fusion(bf16[64,8,1024]{2,1,0:T(8,128)(2,1)} %copy-done.1, bf16[505,1024]{1,0:T(8,128)(2,1)} %copy-done), kind=kOutput, calls=%fused_computation.15 | convolution fusion | flops 528482304 | bytes 3112960 | tf_op jit(solution)/shard_map/dot_general | solution.py:59
  124.3 0.0 copy-start.3
  124.4 1.1 fusion.2
  125.5 12.3 %all-to-all-done.4 = bf16[8,504,128]{2,1,0:T(8,128)(2,1)} async-done(((bf16[8,504,128]{2,1,0:T(8,128)(2,1)}), bf16[8,504,128]{2,1,0:T(8,128)(2,1)}, u32[]{:S(2)}, u32[]{:S(2)}) %all-to-all-start.4) | async-done | bytes 1032224 | tf_op jit(solution)/shard_map/all_to_all | solution.py:75
  137.8 6.7 %all-to-all-start.3 = ((bf16[64,8,512]{2,1,0:T(8,128)(2,1)}), bf16[64,8,512]{2,1,0:T(8,128)(2,1)S(1)}, u32[]{:S(2)}, u32[]{:S(2)}) async-start(bf16[64,8,512]{2,1,0:T(8,128)(2,1)} %fusion.2), calls=%async_computation.3 | async-start | bytes 1048576 | tf_op jit(solution)/shard_map/all_to_all | solution.py:68
  144.5 2.1 %convert_reduce_fusion.1 = f32[504,128]{1,0:T(8,128)} fusion(bf16[8,504,128]{2,1,0:T(8,128)(2,1)} %all-to-all-done.4), kind=kLoop, calls=%fused_computation.3 | loop fusion | flops 967680 | bytes 1290240 | tf_op jit(solution)/shard_map/reduce_sum | solution.py:82
  146.6 17.0 %all-to-all-done.3 = bf16[64,8,512]{2,1,0:T(8,128)(2,1)S(1)} async-done(((bf16[64,8,512]{2,1,0:T(8,128)(2,1)}), bf16[64,8,512]{2,1,0:T(8,128)(2,1)S(1)}, u32[]{:S(2)}, u32[]{:S(2)}) %all-to-all-start.3) | async-done | bytes 524320 | tf_op jit(solution)/shard_map/all_to_all | solution.py:68
  163.6 0.4 convert_select_fusion.1
  164.0 0.2 pad_maximum_fusion
  164.2 1.9 %copy.10 = f32[1024,512]{0,1:T(8,128)} copy(f32[1024,512]{1,0:T(8,128)S(1)} %bitcast.40) | data formatting | bytes 4194304 | tf_op jit(solution)/shard_map/concatenate | solution.py:84
  166.0 2.8 %fusion.7 = bf16[512,1,1024]{2,0,1:T(8,128)(2,1)} fusion(f32[1024,512]{0,1:T(8,128)} %copy.10, f32[512]{0:T(512)S(1)} %bitcast.44), kind=kLoop, calls=%fused_computation.19 | loop fusion | flops 1048576 | bytes 3147776 | tf_op jit(solution)/shard_map/broadcast_in_dim | solution.py:90
  (10 shorter events, 0.0 us)
Async XLA Ops:
  0.6 19.1 %copy-start.2 = (bf16[1,504,128]{2,1,0:T(8,128)(2,1)S(1)}, bf16[1,504,128]{2,1,0:T(8,128)(2,1)}, u32[]{:S(2)}) copy-start(bf16[1,504,128]{2,1,0:T(8,128)(2,1)} %param.7) | copy-start | bytes 387076
  0.7 19.1 %copy-start.4 = (bf16[128]{0:T(256)(128)(2,1)S(1)}, bf16[128]{0:T(256)(128)(2,1)}, u32[]{:S(2)}) copy-start(bf16[128]{0:T(256)(128)(2,1)} %param.8) | copy-start | bytes 772
  3.2 36.0 %all-to-all-start = ((bf16[64,8,512]{2,1,0:T(8,128)(2,1)}), bf16[64,8,512]{2,1,0:T(8,128)(2,1)S(1)}, u32[]{:S(2)}, u32[]{:S(2)}) async-start(bf16[64,8,512]{2,1,0:T(8,128)(2,1)} %broadcast_select_fusion), calls=%async_computation | async-start | bytes 1048576 | tf_op jit(solution)/shard_map/all_to_all | solution.py:23
  34.4 6.8 %copy-start = (bf16[505,1024]{1,0:T(8,128)(2,1)}, bf16[505,1024]{1,0:T(8,128)(2,1)S(1)}, u32[]{:S(2)}) copy-start(bf16[505,1024]{1,0:T(8,128)(2,1)S(1)} %all_gather.3) | copy-start | bytes 3102724
  41.2 37.8 %all-to-all-start.1 = ((bf16[64,8,1024]{2,1,0:T(8,128)(2,1)}), bf16[64,8,1024]{2,1,0:T(8,128)(2,1)S(1)}, u32[]{:S(2)}, u32[]{:S(2)}) async-start(bf16[64,8,1024]{2,1,0:T(8,128)(2,1)} %fusion), calls=%async_computation.1 | async-start | bytes 2097152 | tf_op jit(solution)/shard_map/all_to_all | solution.py:39
  115.9 1.9 %copy-start.1 = (bf16[64,8,1024]{2,1,0:T(8,128)(2,1)}, bf16[64,8,1024]{2,1,0:T(8,128)(2,1)S(1)}, u32[]{:S(2)}) copy-start(bf16[64,8,1024]{2,1,0:T(8,128)(2,1)S(1)} %all_to_all.25) | copy-start | bytes 3145732
  117.8 20.0 %all-to-all-start.4 = ((bf16[8,504,128]{2,1,0:T(8,128)(2,1)}), bf16[8,504,128]{2,1,0:T(8,128)(2,1)}, u32[]{:S(2)}, u32[]{:S(2)}) async-start(bf16[8,504,128]{2,1,0:T(8,128)(2,1)} %bitcast.36), calls=%async_computation.4 | async-start | bytes 2064384 | tf_op jit(solution)/shard_map/all_to_all | solution.py:75
  124.3 20.1 %copy-start.3 = (s32[512,1]{0,1:T(1,128)S(1)}, s32[512,1]{0,1:T(1,128)}, u32[]{:S(2)}) copy-start(s32[512,1]{0,1:T(1,128)} %param.6) | copy-start | bytes 6148
  137.8 25.8 %all-to-all-start.3 = ((bf16[64,8,512]{2,1,0:T(8,128)(2,1)}), bf16[64,8,512]{2,1,0:T(8,128)(2,1)S(1)}, u32[]{:S(2)}, u32[]{:S(2)}) async-start(bf16[64,8,512]{2,1,0:T(8,128)(2,1)} %fusion.2), calls=%async_computation.3 | async-start | bytes 1048576 | tf_op jit(solution)/shard_map/all_to_all | solution.py:68
where the time goes:
time: 170 us; the launch traced here: 169 us
  waiting for transfers between devices  63 us (37%)
  blocking collectives  50.5 us (30%)
  starting transfers between devices  35.5 us (21%)
  other arithmetic  9.48 us (6%)
  matrix products  4.84 us (3%)
  local copies, waits for them, and re-layouts  4.73 us (3%)
    all_to_all x1, blocking collectives, body(): lax.all_to_all(jnp.broadcast_to(own_slope[None], (fields, own_rows, hidde...  35.8 us
    all_to_all x1, waiting for transfers between devices, body(): lax.all_to_all(partial_hidden.astype(bf16).reshape(fields, own_rows, hidd...  29 us
    all_to_all x1, waiting for transfers between devices, body(): lax.all_to_all((dense_grad * mine_wide).astype(bf16), 'field', split_axis...  17 us
    all_to_all x1, starting transfers between devices, body(): lax.all_to_all(outbound, 'field', split_axis=0, concat_axis=0, tiled=True)  16.6 us
    all_gather x1, blocking collectives, body(): lax.all_gather(jnp.concatenate([w_pairs[0], bias_rows], 0), 'batch', axis...  14.6 us
    all_to_all x1, waiting for transfers between devices, body(): lax.all_to_all(weight_term.reshape(pair_count, shards, unit_cols).transpo...  12.3 us
    all_to_all x1, starting transfers between devices, body(): lax.all_to_all(partial_hidden.astype(bf16).reshape(fields, own_rows, hidd...  8.01 us
    all_to_all x1, starting transfers between devices, body(): lax.all_to_all((dense_grad * mine_wide).astype(bf16), 'field', split_axis...  6.67 us
  transfers between devices with their start and end apart: 4, of which 4 were waited for; matrix products, arithmetic and copies ran while one was open for 4% of the time, Pallas kernels for 0%

commit v1 on v0

--- a/solution.py
+++ b/solution.py
@@ -22,8 +22,14 @@
     outbound = jnp.where(upper_half, embedded[:, :half_depth], embedded[:, half_depth:])
     received = lax.all_to_all(outbound, "field", split_axis=0, concat_axis=0, tiled=True)
     bias_rows = jnp.pad(bias_terms[None, :], ((0, 0), (0, 0)))
-    weight_bias = lax.all_gather(
-        jnp.concatenate([w_pairs[0], bias_rows], 0), "batch", axis=1, tiled=True
+    weight_bias = jnp.concatenate(
+        lax.all_to_all(
+            jnp.stack([jnp.concatenate([w_pairs[0], bias_rows], 0)] * lax.axis_size("batch")),
+            "batch",
+            0,
+            0,
+        ),
+        axis=1,
     )
     weight_cols = weight_bias[:pair_count]
     bias_float = weight_bias[pair_count].astype(f32)

time: 170 us -> 187 us (1.10)
  waiting for transfers between devices: 63 us -> 84.6 us
  blocking collectives: 50.5 us -> 34.6 us
  local copies, waits for them, and re-layouts: 4.73 us -> 11.8 us
  other arithmetic: 9.48 us -> 11.7 us
    all_gather x1 -> x0, blocking collectives: 14.6 us -> none  [body(): lax.all_gather(jnp.concatenate([w_pairs[0], bias_rows], 0), 'batch', axis...]
    all_to_all x0 -> x1, waiting for transfers between devices: none -> 14.5 us  [body(): lax.all_to_all(jnp.stack([jnp.concatenate([w_pairs[0], bias_rows], 0)] *...]
    all_to_all x1, waiting for transfers between devices: 4.7 us -> 16.5 us  [body(): lax.all_to_all(outbound, 'field', split_axis=0, concat_axis=0, tiled=True)]
    all_to_all x0 -> x1, starting transfers between devices: none -> 4.3 us  [body(): lax.all_to_all(jnp.stack([jnp.concatenate([w_pairs[0], bias_rows], 0)] *...]
    slice x0 -> x3, local copies, waits for them, and re-layouts: none -> 3.73 us  [body(): weight_cols = weight_bias[:pair_count]]
    all_to_all x1, waiting for transfers between devices: 12.3 us -> 8.9 us  [body(): lax.all_to_all(weight_term.reshape(pair_count, shards, unit_cols).transpo...]
    all_to_all x1, starting transfers between devices: 8.01 us -> 5.62 us  [body(): lax.all_to_all(partial_hidden.astype(bf16).reshape(fields, own_rows, hidd...]
    dot_general x0 -> x1, local copies, waits for them, and re-layouts: none -> 2.31 us  [body(): lax.dot_general(weight_cols, slope_act, (((1,), (1,)), ((), ())), preferr...]
  transfers between devices with their start and end apart: 4 -> 5, of which waited for: 4 -> 5; matrix products, arithmetic and copies ran while one was open for 4% -> 7% of each run, Pallas kernels for 0% -> 0%
where the time goes in v1:
time: 187 us; the launch traced here: 186 us
  waiting for transfers between devices  84.6 us (45%)
  starting transfers between devices  37.3 us (20%)
  blocking collectives  34.6 us (19%)
  local copies, waits for them, and re-layouts  11.8 us (6%)
  other arithmetic  11.7 us (6%)
  matrix products  4.92 us (3%)
    all_to_all x1, blocking collectives, body(): lax.all_to_all(jnp.broadcast_to(own_slope[None], (fields, own_rows, hidde...  34.6 us
    all_to_all x1, waiting for transfers between devices, body(): lax.all_to_all(partial_hidden.astype(bf16).reshape(fields, own_rows, hidd...  27.7 us
    all_to_all x1, waiting for transfers between devices, body(): lax.all_to_all((dense_grad * mine_wide).astype(bf16), 'field', split_axis...  17 us
    all_to_all x1, starting transfers between devices, body(): lax.all_to_all(outbound, 'field', split_axis=0, concat_axis=0, tiled=True)  16.6 us
    all_to_all x1, waiting for transfers between devices, body(): lax.all_to_all(outbound, 'field', split_axis=0, concat_axis=0, tiled=True)  16.5 us
    all_to_all x1, waiting for transfers between devices, body(): lax.all_to_all(jnp.stack([jnp.concatenate([w_pairs[0], bias_rows], 0)] *...  14.5 us
    all_to_all x1, waiting for transfers between devices, body(): lax.all_to_all(weight_term.reshape(pair_count, shards, unit_cols).transpo...  8.9 us
    all_to_all x1, starting transfers between devices, body(): lax.all_to_all((dense_grad * mine_wide).astype(bf16), 'field', split_axis...  6.55 us
  transfers between devices with their start and end apart: 5, of which 5 were waited for; matrix products, arithmetic and copies ran while one was open for 7% of the time, Pallas kernels for 0%

profile of v1, /device:TPU:8, one launch (start us, length us, event | category | flops | bytes accessed | tf_op | source)
XLA Modules:
  0.0 185.8 jit_solution(172808702459877028)
XLA Ops:
  0.6 1.0 pad_maximum_fusion.1
  1.7 1.1 stack.2
  2.8 4.3 %all-to-all-start = ((bf16[8,505,128]{2,1,0:T(8,128)(2,1)}), bf16[8,505,128]{2,1,0:T(8,128)(2,1)}, u32[]{:S(2)}, u32[]{:S(2)}) async-start(bf16[8,505,128]{2,1,0:T(8,128)(2,1)} %stack.2), calls=%async_computation | async-start | bytes 2097152 | tf_op jit(solution)/shard_map/all_to_all | solution.py:26
  7.1 0.5 copy.14
  7.6 1.0 broadcast_select_fusion
  8.6 14.5 %all-to-all-done = bf16[8,505,128]{2,1,0:T(8,128)(2,1)} async-done(((bf16[8,505,128]{2,1,0:T(8,128)(2,1)}), bf16[8,505,128]{2,1,0:T(8,128)(2,1)}, u32[]{:S(2)}, u32[]{:S(2)}) %all-to-all-start) | async-done | bytes 1034272 | tf_op jit(solution)/shard_map/all_to_all | solution.py:26
  23.1 16.6 %all-to-all-start.1 = ((bf16[64,8,512]{2,1,0:T(8,128)(2,1)}), bf16[64,8,512]{2,1,0:T(8,128)(2,1)S(1)}, u32[]{:S(2)}, u32[]{:S(2)}) async-start(bf16[64,8,512]{2,1,0:T(8,128)(2,1)} %broadcast_select_fusion), calls=%async_computation.1 | async-start | bytes 1048576 | tf_op jit(solution)/shard_map/all_to_all | solution.py:23
  39.7 1.3 slice.31
  41.0 1.3 copy.15
  42.3 16.5 %all-to-all-done.1 = bf16[64,8,512]{2,1,0:T(8,128)(2,1)S(1)} async-done(((bf16[64,8,512]{2,1,0:T(8,128)(2,1)}), bf16[64,8,512]{2,1,0:T(8,128)(2,1)S(1)}, u32[]{:S(2)}, u32[]{:S(2)}) %all-to-all-start.1) | async-done | bytes 524320 | tf_op jit(solution)/shard_map/all_to_all | solution.py:23
  59.1 1.0 copy-done.2
  60.0 1.9 %fusion = bf16[64,8,1024]{2,1,0:T(8,128)(2,1)} fusion(bf16[504,1024]{0,1:T(8,128)(2,1)S(1)} %bitcast.43, bf16[64,8,512]{2,1,0:T(8,128)(2,1)S(1)} %fusion.3, pred[63]{0:T(512)(128)(4,1)S(1)} %iota_compare_fusion.1), kind=kOutput, calls=%fused_computation.6 | convolution fusion | flops 529264640 | bytes 3129856 | tf_op jit(solution)/shard_map/dot_general | solution.py:42
  61.9 5.6 %all-to-all-start.2 = ((bf16[64,8,1024]{2,1,0:T(8,128)(2,1)}), bf16[64,8,1024]{2,1,0:T(8,128)(2,1)}, u32[]{:S(2)}, u32[]{:S(2)}) async-start(bf16[64,8,1024]{2,1,0:T(8,128)(2,1)} %fusion), calls=%async_computation.2 | async-start | bytes 2097152 | tf_op jit(solution)/shard_map/all_to_all | solution.py:45
  67.5 0.7 slice_convert_fusion
  68.3 27.7 %all-to-all-done.2 = bf16[64,8,1024]{2,1,0:T(8,128)(2,1)} async-done(((bf16[64,8,1024]{2,1,0:T(8,128)(2,1)}), bf16[64,8,1024]{2,1,0:T(8,128)(2,1)}, u32[]{:S(2)}, u32[]{:S(2)}) %all-to-all-start.2) | async-done | bytes 1048608 | tf_op jit(solution)/shard_map/all_to_all | solution.py:45
  96.0 1.4 convert_reduce_fusion
  97.4 0.7 multiply_convert_fusion
  98.3 34.6 %all_to_all.30 = bf16[64,8,1024]{2,1,0:T(8,128)(2,1)S(1)} all-to-all(bf16[64,8,1024]{2,1,0:T(8,128)(2,1)S(1)} %broadcast_in_dim.66), channel_id=1, replica_groups=mesh['field'=64,'batch'=8] {'field'}, dimensions={0} | all-to-all | bytes 2097152 | tf_op jit(solution)/shard_map/all_to_all | solution.py:58
  132.9 0.7 fusion.1
  133.7 1.2 copy.20
  134.9 4.2 %all-to-all-start.5 = ((bf16[8,504,128]{2,1,0:T(8,128)(2,1)}), bf16[8,504,128]{2,1,0:T(8,128)(2,1)}, u32[]{:S(2)}, u32[]{:S(2)}) async-start(bf16[8,504,128]{2,1,0:T(8,128)(2,1)} %bitcast.42), calls=%async_computation.5 | async-start | bytes 2064384 | tf_op jit(solution)/shard_map/all_to_all | solution.py:81
  139.1 1.1 copy.13
  140.3 2.3 %dot_general.11 = bf16[63,8,1024]{2,1,0:T(8,128)(2,1)} reshape(bf16[504,8,128]{2,1,0:T(8,128)(2,1)} %copy.13) | data formatting | bytes 2064384 | tf_op jit(solution)/shard_map/dot_general | solution.py:65
  142.6 2.3 %fusion.4 = f32[63,8,512]{2,1,0:T(8,128)S(1)} fusion(bf16[63,8,1024]{2,1,0:T(8,128)(2,1)} %dot_general.11, bf16[64,8,1024]{2,1,0:T(8,128)(2,1)} %copy-done.1), kind=kOutput, calls=%fused_computation.15 | convolution fusion | flops 528482304 | bytes 3112960 | tf_op jit(solution)/shard_map/dot_general | solution.py:65
  144.9 1.1 fusion.2
  146.0 8.9 %all-to-all-done.5 = bf16[8,504,128]{2,1,0:T(8,128)(2,1)} async-done(((bf16[8,504,128]{2,1,0:T(8,128)(2,1)}), bf16[8,504,128]{2,1,0:T(8,128)(2,1)}, u32[]{:S(2)}, u32[]{:S(2)}) %all-to-all-start.5) | async-done | bytes 1032224 | tf_op jit(solution)/shard_map/all_to_all | solution.py:81
  154.9 6.5 %all-to-all-start.4 = ((bf16[64,8,512]{2,1,0:T(8,128)(2,1)}), bf16[64,8,512]{2,1,0:T(8,128)(2,1)S(1)}, u32[]{:S(2)}, u32[]{:S(2)}) async-start(bf16[64,8,512]{2,1,0:T(8,128)(2,1)} %fusion.2), calls=%async_computation.4 | async-start | bytes 1048576 | tf_op jit(solution)/shard_map/all_to_all | solution.py:74
  161.5 2.1 %convert_reduce_fusion.1 = f32[504,128]{1,0:T(8,128)} fusion(bf16[8,504,128]{2,1,0:T(8,128)(2,1)} %all-to-all-done.5), kind=kLoop, calls=%fused_computation.3 | loop fusion | flops 967680 | bytes 1290240 | tf_op jit(solution)/shard_map/reduce_sum | solution.py:88
  163.5 17.0 %all-to-all-done.4 = bf16[64,8,512]{2,1,0:T(8,128)(2,1)S(1)} async-done(((bf16[64,8,512]{2,1,0:T(8,128)(2,1)}), bf16[64,8,512]{2,1,0:T(8,128)(2,1)S(1)}, u32[]{:S(2)}, u32[]{:S(2)}) %all-to-all-start.4) | async-done | bytes 524320 | tf_op jit(solution)/shard_map/all_to_all | solution.py:74
  180.5 0.4 convert_select_fusion.1
  181.1 1.9 %copy.16 = f32[1024,512]{0,1:T(8,128)} copy(f32[1024,512]{1,0:T(8,128)S(1)} %bitcast.41) | data formatting | bytes 4194304 | tf_op jit(solution)/shard_map/concatenate | solution.py:90
  183.0 2.8 %fusion.7 = bf16[512,1,1024]{2,0,1:T(8,128)(2,1)} fusion(f32[1024,512]{0,1:T(8,128)} %copy.16, f32[512]{0:T(512)S(1)} %bitcast.47), kind=kLoop, calls=%fused_computation.19 | loop fusion | flops 1048576 | bytes 3147776 | tf_op jit(solution)/shard_map/broadcast_in_dim | solution.py:96
  (14 shorter events, 0.6 us)
Async XLA Ops:
  0.6 6.4 %copy-start = (bf16[512,1,1024]{2,0,1:T(8,128)(2,1)S(1)}, bf16[512,1,1024]{2,0,1:T(8,128)(2,1)}, u32[]{:S(2)}) copy-start(bf16[512,1,1024]{2,0,1:T(8,128)(2,1)} %param.5) | copy-start | bytes 3145732
  2.8 20.3 %all-to-all-start = ((bf16[8,505,128]{2,1,0:T(8,128)(2,1)}), bf16[8,505,128]{2,1,0:T(8,128)(2,1)}, u32[]{:S(2)}, u32[]{:S(2)}) async-start(bf16[8,505,128]{2,1,0:T(8,128)(2,1)} %stack.2), calls=%async_computation | async-start | bytes 2097152 | tf_op jit(solution)/shard_map/all_to_all | solution.py:26
  23.1 35.7 %all-to-all-start.1 = ((bf16[64,8,512]{2,1,0:T(8,128)(2,1)}), bf16[64,8,512]{2,1,0:T(8,128)(2,1)S(1)}, u32[]{:S(2)}, u32[]{:S(2)}) async-start(bf16[64,8,512]{2,1,0:T(8,128)(2,1)} %broadcast_select_fusion), calls=%async_computation.1 | async-start | bytes 1048576 | tf_op jit(solution)/shard_map/all_to_all | solution.py:23
  58.8 1.2 copy-start.2
  61.9 34.1 %all-to-all-start.2 = ((bf16[64,8,1024]{2,1,0:T(8,128)(2,1)}), bf16[64,8,1024]{2,1,0:T(8,128)(2,1)}, u32[]{:S(2)}, u32[]{:S(2)}) async-start(bf16[64,8,1024]{2,1,0:T(8,128)(2,1)} %fusion), calls=%async_computation.2 | async-start | bytes 2097152 | tf_op jit(solution)/shard_map/all_to_all | solution.py:45
  132.9 2.0 %copy-start.1 = (bf16[64,8,1024]{2,1,0:T(8,128)(2,1)}, bf16[64,8,1024]{2,1,0:T(8,128)(2,1)S(1)}, u32[]{:S(2)}) copy-start(bf16[64,8,1024]{2,1,0:T(8,128)(2,1)S(1)} %all_to_all.30) | copy-start | bytes 3145732
  134.9 20.0 %all-to-all-start.5 = ((bf16[8,504,128]{2,1,0:T(8,128)(2,1)}), bf16[8,504,128]{2,1,0:T(8,128)(2,1)}, u32[]{:S(2)}, u32[]{:S(2)}) async-start(bf16[8,504,128]{2,1,0:T(8,128)(2,1)} %bitcast.42), calls=%async_computation.5 | async-start | bytes 2064384 | tf_op jit(solution)/shard_map/all_to_all | solution.py:81
  144.8 16.6 %copy-start.3 = (s32[512,1]{0,1:T(1,128)S(1)}, s32[512,1]{0,1:T(1,128)}, u32[]{:S(2)}) copy-start(s32[512,1]{0,1:T(1,128)} %param.6) | copy-start | bytes 6148
  154.9 25.6 %all-to-all-start.4 = ((bf16[64,8,512]{2,1,0:T(8,128)(2,1)}), bf16[64,8,512]{2,1,0:T(8,128)(2,1)S(1)}, u32[]{:S(2)}, u32[]{:S(2)}) async-start(bf16[64,8,512]{2,1,0:T(8,128)(2,1)} %fusion.2), calls=%async_computation.4 | async-start | bytes 1048576 | tf_op jit(solution)/shard_map/all_to_all | solution.py:74
